TPU v7x, 256 devices: a whole 4x4x8 slice. The times are simulated.
256 devices in a mesh: wide: 32 (over x, z), narrow: 8 (over y, core).
Axes of the slice: x: 4, y: 4, z: 8, core: 2. Of those that a mesh axis runs over, the one named last changes fastest.
Arguments:
- hidden_in: bfloat16 [16384, 1664], P(('wide', 'narrow')), may hold values from -3 to 3
- queries: bfloat16 [16, 1024, 1664], P('narrow', 'wide'), may hold values from -24 to 24
- keys: bfloat16 [16, 1024, 1664], P('narrow', 'wide'), may hold values from -24 to 24
- values: bfloat16 [16, 1024, 1664], P('narrow', 'wide'), may hold values from -12 to 12
- out_weight: bfloat16 [1664, 1664], P('narrow', 'wide'), may hold values from -0.25 to 0.25
- merge_weight: bfloat16 [4, 1664, 1664], P(None, 'narrow', 'wide'), may hold values from -0.125 to 0.125
- segment_ids: int32 [4096], P('wide'), may hold values from 0 to 15, never falling along the last dimension, each value on 1 to 2560 neighbouring positions
- owners: int32 [4096, 1], P('wide'), may hold values from 0 to 31; in each aligned block of 128 rows (0 to 127, 128 to 255, ...) at most 8 rows name the same one
Outputs:
- hidden_out: bfloat16 [16384, 1664], P(('wide', 'narrow'))
- delivered: bfloat16 [8192, 1664], P('wide', 'narrow')
Inputs may be any that keep to these rules, and one draw needn't show every extreme that they name: `segment_ids`: never falling along the tokens; the largest image or clip holds exactly 2560 merged tokens. `owners`: among the merged tokens of one index of wide, at most 8 share an owner, and exactly 8 do for some owner.
All inputs are finite; a program needn't handle non-finite values.
Results may differ from a plain program's by a relative error of at most 0.025.
Values may be sent and summed in bfloat16 or wider, within the bound.
A program may use at most 64 MiB of HBM per device.

v0:
```python
import math
import jax
import jax.numpy as jnp
from jax import lax
from jax.sharding import PartitionSpec as P

HEAD_DIM = 104
NEG = -1e30


def shards(hidden_in, queries, keys, values, out_weight, merge_weight, segment_ids, owners):
    heads_here, packed_rows, packed_width = queries.shape
    tok_rows = packed_rows * 16
    local_width = heads_here * HEAD_DIM
    scale = 1.0 / math.sqrt(HEAD_DIM)
    tok_seg = jnp.repeat(segment_ids, 4)
    seg_packed = tok_seg.reshape(1, packed_rows, 16)
    gathered_out, gathered_merge = (
        lax.all_gather(out_weight, "wide", axis=1, tiled=True),
        lax.all_gather(merge_weight, "wide", axis=2, tiled=True),
    )
    query_heads = queries.reshape(heads_here, tok_rows, HEAD_DIM)

    def key_block(carry, key_rows, value_rows, seg_rows):
        keep = tok_seg[:, None] == seg_rows[None, :]
        best, total, accum = carry
        key_heads = key_rows.reshape(heads_here, -1, HEAD_DIM)
        value_heads = value_rows.reshape(heads_here, -1, HEAD_DIM)
        scores = (
            jnp.einsum("hqd,hkd->hqk", query_heads, key_heads, preferred_element_type=jnp.float32)
            * scale
        )
        scores = jnp.where(keep[None], scores, NEG)
        new_best = jnp.maximum(best, jnp.max(scores, axis=-1))
        weights = jnp.where(keep[None], jnp.exp(scores - new_best[..., None]), 0.0)
        factor = jnp.exp(best - new_best)
        total = total * factor + jnp.sum(weights, axis=-1)
        accum = accum * factor[..., None] + jnp.einsum(
            "hqk,hkd->hqd",
            weights.astype(jnp.bfloat16),
            value_heads,
            preferred_element_type=jnp.float32,
        )
        return (new_best, total, accum)

    start_state = (
        jnp.full((heads_here, tok_rows), NEG, jnp.float32),
        jnp.zeros((heads_here, tok_rows), jnp.float32),
        jnp.zeros((heads_here, tok_rows, HEAD_DIM), jnp.float32),
    )
    carry = start_state
    key_rows = lax.all_gather(keys, "wide", axis=1, tiled=True)
    value_rows = lax.all_gather(values, "wide", axis=1, tiled=True)
    seg_rows = lax.all_gather(seg_packed, "wide", axis=1, tiled=True)
    count = key_rows.shape[1]
    blocks = count // 32
    stacked = (
        key_rows.reshape(heads_here, blocks, 32, packed_width).transpose(1, 0, 2, 3),
        value_rows.reshape(heads_here, blocks, 32, packed_width).transpose(1, 0, 2, 3),
        seg_rows.reshape(blocks, 512),
    )

    def step_block(state, item):
        return (key_block(state, item[0], item[1], item[2]), None)

    carry, unused = lax.scan(step_block, carry, stacked)
    best, total, accum = carry
    attn = (
        (accum / total[..., None])
        .transpose(1, 0, 2)
        .reshape(tok_rows, local_width)
        .astype(jnp.bfloat16)
    )
    partial_mix = jnp.dot(attn, gathered_out, preferred_element_type=jnp.float32)
    summed_mix = lax.psum_scatter(
        partial_mix.astype(jnp.bfloat16), "narrow", scatter_dimension=0, tiled=True
    ).astype(jnp.float32)
    hidden_out = (hidden_in.astype(jnp.float32) + summed_mix).astype(jnp.bfloat16)
    whole_rows = lax.all_gather(hidden_out, "narrow", axis=0, tiled=True)
    my_columns = lax.dynamic_slice_in_dim(
        whole_rows, lax.axis_index("narrow") * local_width, local_width, 1
    )
    merged_rows = tok_rows // 4
    grouped = my_columns.reshape(merged_rows, 4, local_width)
    partial_feat = jnp.einsum(
        "gjc,jco->go", grouped, gathered_merge, preferred_element_type=jnp.float32
    )
    feature = lax.psum_scatter(
        partial_feat.astype(jnp.bfloat16), "narrow", scatter_dimension=1, tiled=True
    )
    owner_count = lax.axis_size("wide")
    capacity = 2 * merged_rows // owner_count
    owner_col = owners[:, 0]
    onehot = (owner_col[:, None] == jnp.arange(owner_count, dtype=jnp.int32)[None, :]).astype(
        jnp.int32
    )
    rank = jnp.sum(jnp.cumsum(onehot, axis=0) * onehot, axis=1) - 1
    slot = owner_col * capacity + rank
    picker = (jnp.arange(owner_count * capacity, dtype=jnp.int32)[:, None] == slot[None, :]).astype(
        jnp.bfloat16
    )
    outgoing = jnp.dot(picker, feature, preferred_element_type=jnp.float32).astype(jnp.bfloat16)
    outgoing = outgoing.reshape(owner_count, capacity, feature.shape[1])
    arrived = lax.all_to_all(outgoing, "wide", split_axis=0, concat_axis=0, tiled=True)
    return (hidden_out, arrived.reshape(owner_count * capacity, feature.shape[1]))


def solution(mesh):
    return jax.shard_map(
        shards,
        mesh=mesh,
        in_specs=(
            P(("wide", "narrow"), None),
            P("narrow", "wide", None),
            P("narrow", "wide", None),
            P("narrow", "wide", None),
            P("narrow", "wide"),
            P(None, "narrow", "wide"),
            P("wide"),
            P("wide", None),
        ),
        out_specs=(P(("wide", "narrow"), None), P("wide", "narrow")),
        check_vma=False,
    )
```

profile of v0, /device:TPU:32, one launch (start us, length us, event | category | flops | bytes accessed | tf_op | source)
XLA Modules:
  0.0 576.4 jit_solution(16896971549550113275)
XLA Ops:
  9.7 51.9 %all_gather.18 = s32[1,1024,16]{2,0,1:T(1,128)S(1)} all-gather(s32[1,32,16]{2,0,1:T(1,128)S(1)} %copy.25), channel_id=1, replica_groups=mesh['wide'=32,'narrow'=8] {'wide'}, dimensions={1}, use_global_device_ids=true | all-gather | bytes 67584 | tf_op jit(solution)/shard_map/all_gather | solution.py:54
  62.1 2.0 reduce.3
  65.1 49.1 %all-gather = bf16[32,52,208]{2,1,0:T(8,128)(2,1)S(1)} all-gather(bf16[1,52,208]{2,1,0:T(8,128)(2,1)S(1)} %bitcast.77), channel_id=1, replica_groups=mesh['wide'=32,'narrow'=8] {'wide'}, dimensions={0}, use_global_device_ids=true | all-gather | bytes 713856 | tf_op jit(solution)/shard_map/all_gather | solution.py:19
  114.2 1.3 reshape.93
  115.5 82.9 %all-gather.8.cloned.1.call-done = bf16[2,1024,1664]{2,1,0:T(8,128)(2,1)} async-done(((bf16[2,32,1664]{2,1,0:T(8,128)(2,1)}), bf16[2,1024,1664]{2,1,0:T(8,128)(2,1)}) %all-gather.8.cloned.1.call-update) | async-done | bytes 6815760 | tf_op jit(solution)/shard_map/all_gather | solution.py:53
  198.4 167.4 %while.15 = (s32[]{:T(128)}, f32[2,512]{1,0:T(2,128)S(1)}, f32[2,512]{1,0:T(2,128)S(1)}, f32[2,512,104]{1,2,0:T(8,128)S(1)}, s32[32,512]{1,0:T(8,128)S(1)}, /*in...) while((s32[]{:T(128)}, f32[2,512]{1,0:T(2,128)S(1)}, ...), condition=%wide.region_3.4_spmd.clone, body=%wide.region_0.3_spmd.clone.sunk | while | flops 225506304 | bytes 10615425 | solution.py:66
  199.5 1.1 dynamic-slice_bitcast_fusion.3
  204.7 1.1 dynamic-slice_bitcast_fusion.3
  209.9 1.1 dynamic-slice_bitcast_fusion.3
  215.2 1.1 dynamic-slice_bitcast_fusion.3
  220.4 1.1 dynamic-slice_bitcast_fusion.3
  225.6 1.1 dynamic-slice_bitcast_fusion.3
  230.9 1.1 dynamic-slice_bitcast_fusion.3
  236.1 1.1 dynamic-slice_bitcast_fusion.3
  241.3 1.1 dynamic-slice_bitcast_fusion.3
  246.6 1.1 dynamic-slice_bitcast_fusion.3
  251.8 1.1 dynamic-slice_bitcast_fusion.3
  257.0 1.1 dynamic-slice_bitcast_fusion.3
  262.3 1.1 dynamic-slice_bitcast_fusion.3
  267.5 1.1 dynamic-slice_bitcast_fusion.3
  272.7 1.1 dynamic-slice_bitcast_fusion.3
  278.0 1.1 dynamic-slice_bitcast_fusion.3
  283.2 1.1 dynamic-slice_bitcast_fusion.3
  288.4 1.1 dynamic-slice_bitcast_fusion.3
  293.7 1.1 dynamic-slice_bitcast_fusion.3
  298.9 1.1 dynamic-slice_bitcast_fusion.3
  304.1 1.1 dynamic-slice_bitcast_fusion.3
  309.4 1.1 dynamic-slice_bitcast_fusion.3
  314.6 1.1 dynamic-slice_bitcast_fusion.3
  319.8 1.1 dynamic-slice_bitcast_fusion.3
  325.1 1.1 dynamic-slice_bitcast_fusion.3
  330.3 1.1 dynamic-slice_bitcast_fusion.3
  335.5 1.1 dynamic-slice_bitcast_fusion.3
  340.7 1.1 dynamic-slice_bitcast_fusion.3
  346.0 1.1 dynamic-slice_bitcast_fusion.3
  351.2 1.1 dynamic-slice_bitcast_fusion.3
  356.4 1.1 dynamic-slice_bitcast_fusion.3
  361.7 1.1 dynamic-slice_bitcast_fusion.3
  365.9 3.1 convolution_convert_fusion
  369.0 33.3 %reduce-scatter.5.cloned.1.call-done = bf16[64,1664]{1,0:T(8,128)(2,1)} async-done(((bf16[512,1664]{1,0:T(8,128)(2,1)}), bf16[64,1664]{1,0:T(8,128)(2,1)}) %reduce-scatter.5.cloned.1.call-update) | async-done | bytes 213008 | tf_op jit(solution)/shard_map/reduce_scatter | solution.py:75
  402.4 1.7 add_convert_fusion
  404.7 26.0 %all-gather.10.cloned.1.call-done = bf16[512,1664]{1,0:T(8,128)(2,1)} async-done(((bf16[64,1664]{1,0:T(8,128)(2,1)}), bf16[512,1664]{1,0:T(8,128)(2,1)}) %all-gather.10.cloned.1.call-update) | async-done | bytes 1703952 | tf_op jit(solution)/shard_map/all_gather | solution.py:79
  430.8 1.1 constant_dynamic-slice_fusion.1
  432.0 81.6 %all-gather.12.cloned.1.call-done = bf16[4,208,1664]{1,0,2:T(4,128)(2,1)} async-done(((bf16[4,208,52]{1,0,2:T(4,128)(2,1)}), bf16[4,208,1664]{1,0,2:T(4,128)(2,1)}) %all-gather.12.cloned.1.call-update) | async-done | bytes 2768912 | tf_op jit(solution)/shard_map/all_gather | solution.py:20
  513.6 3.8 fusion.23
  517.9 30.2 %reduce-scatter.7.cloned.1.call-done = bf16[208,128]{1,0:T(8,128)(2,1)} async-done(((bf16[1664,128]{1,0:T(8,128)(2,1)}), bf16[208,128]{1,0:T(8,128)(2,1)}) %reduce-scatter.7.cloned.1.call-update) | async-done | bytes 53264
  548.1 1.0 convolution_convert_fusion.1
  549.2 19.6 %all_to_all.5 = bf16[32,8,208]{2,1,0:T(8,128)(2,1)S(1)} all-to-all(bf16[32,8,208]{2,1,0:T(8,128)(2,1)S(1)} %bitcast.71), channel_id=1, replica_groups=mesh['wide'=32,'narrow'=8] {'wide'}, dimensions={0} | all-to-all | bytes 212992 | tf_op jit(solution)/shard_map/all_to_all | solution.py:104
  (424 shorter events, 136.0 us)
Async XLA Ops:
  7.2 57.2 %copy-start.1 = (bf16[2,32,1664]{2,1,0:T(8,128)(2,1)S(1)}, bf16[2,32,1664]{2,1,0:T(8,128)(2,1)}, u32[]{:S(2)}) copy-start(bf16[2,32,1664]{2,1,0:T(8,128)(2,1)} %param.11) | copy-start | bytes 638980
  7.2 57.9 %copy-start.2 = (bf16[208,52]{0,1:T(8,128)(2,1)S(1)}, bf16[208,52]{0,1:T(8,128)(2,1)}, u32[]{:S(2)}) copy-start(bf16[208,52]{0,1:T(8,128)(2,1)} %param.14) | copy-start | bytes 64900
  7.2 108.3 %all-gather.6.cloned.1.call-start = ((), (), s32[]{:S(2)}) async-start(), calls=%async_computation.3 | async-start | bytes 7028736 | tf_op jit(solution)/shard_map/all_gather | solution.py:52
  7.9 190.5 %all-gather.8.cloned.1.call-start = ((), (), s32[]{:S(2)}) async-start(), calls=%async_computation.4 | async-start | bytes 7028736 | tf_op jit(solution)/shard_map/all_gather | solution.py:53
  8.7 393.7 %reduce-scatter.5.cloned.1.call-start = ((), (), s32[]{:S(2)}) async-start(), calls=%async_computation.5 | async-start | bytes 1916928 | tf_op jit(solution)/shard_map/reduce_scatter | solution.py:75
  365.9 36.5 %copy-start = (bf16[64,1664]{1,0:T(8,128)(2,1)S(1)}, bf16[64,1664]{1,0:T(8,128)(2,1)}, u32[]{:S(2)}) copy-start(bf16[64,1664]{1,0:T(8,128)(2,1)} %param.10) | copy-start | bytes 638980
  369.0 61.8 %all-gather.10.cloned.1.call-start = ((), (), s32[]{:S(2)}) async-start(), calls=%async_computation.6 | async-start | bytes 1916928 | tf_op jit(solution)/shard_map/all_gather | solution.py:79
  404.1 109.6 %all-gather.12.cloned.1.call-start = ((), (), s32[]{:S(2)}) async-start(), calls=%async_computation.7 | async-start | bytes 3514368 | tf_op jit(solution)/shard_map/all_gather | solution.py:20
  404.7 143.5 %reduce-scatter.7.cloned.1.call-start = ((), (), s32[]{:S(2)}) async-start(), calls=%async_computation.8 | async-start | bytes 479232
  432.0 85.4 %copy-start.3 = (s32[128,1]{0,1:T(1,128)S(1)}, s32[128,1]{0,1:T(1,128)}, u32[]{:S(2)}) copy-start(s32[128,1]{0,1:T(1,128)} %param.17) | copy-start | bytes 1540
Sparse Core Ops, SparseCore 0:
  10.6 96.3 all-gather.5
  109.6 88.7 all-gather.7
  369.1 33.2 reduce-scatter.4
  404.8 25.9 all-gather.9
  433.5 80.0 all-gather.11
  517.5 30.5 reduce-scatter.6
where the time goes:
time: 578 us; the launch traced here: 576 us
  waiting for transfers between devices  256 us (44%)
  blocking collectives  121 us (21%)
  local copies, waits for them, and re-layouts  101 us (17%)
  matrix products  50.9 us (9%)
  other arithmetic  30.1 us (5%)
  between operations  14.3 us (2%)
    all_gather x1, waiting for transfers between devices, shards(): value_rows = lax.all_gather(values, 'wide', axis=1, tiled=True)  82.9 us
    all_gather x1, waiting for transfers between devices, shards(): lax.all_gather(merge_weight, 'wide', axis=2, tiled=True)  81.6 us
    all_gather x1, blocking collectives, shards(): seg_rows = lax.all_gather(seg_packed, 'wide', axis=1, tiled=True)  51.9 us
    all_gather x1, blocking collectives, shards(): lax.all_gather(out_weight, 'wide', axis=1, tiled=True)  49.1 us
    dynamic_slice x64, local copies, waits for them, and re-layouts, shards(): carry, unused = lax.scan(step_block, carry, stacked)  34.9 us
    reduce_scatter x1, waiting for transfers between devices, shards(): lax.psum_scatter(partial_mix.astype(jnp.bfloat16), 'narrow', scatter_dime...  33.3 us
    unnamed x7, waiting for transfers between devices  32.2 us
    all_gather x1, waiting for transfers between devices, shards(): whole_rows = lax.all_gather(hidden_out, 'narrow', axis=0, tiled=True)  26 us
  transfers between devices with their start and end apart: 6, of which 5 were waited for; matrix products, arithmetic and copies ran while one was open for 1% of the time, Pallas kernels for 0%

commit v1 on v0

--- a/solution.py
+++ b/solution.py
@@ -76,7 +76,14 @@
         partial_mix.astype(jnp.bfloat16), "narrow", scatter_dimension=0, tiled=True
     ).astype(jnp.float32)
     hidden_out = (hidden_in.astype(jnp.float32) + summed_mix).astype(jnp.bfloat16)
-    whole_rows = lax.all_gather(hidden_out, "narrow", axis=0, tiled=True)
+    ring = [hidden_out]
+    for hop in range(7):
+        ring.append(lax.ppermute(ring[-1], "narrow", [(dev, (dev + 1) % 8) for dev in range(8)]))
+    whole_rows = jnp.roll(
+        jnp.concatenate(ring[::-1], axis=0),
+        (lax.axis_index("narrow") + 1) * ring[0].shape[0],
+        axis=0,
+    )
     my_columns = lax.dynamic_slice_in_dim(
         whole_rows, lax.axis_index("narrow") * local_width, local_width, 1
     )

time: 578 us -> 547 us (0.946)
  waiting for transfers between devices: 256 us -> 227 us
    all_gather x1, waiting for transfers between devices: 81.6 us -> 34.3 us  [shards(): lax.all_gather(merge_weight, 'wide', axis=2, tiled=True)]
    ppermute x0 -> x7, waiting for transfers between devices: none -> 45.3 us  [shards(): lax.ppermute(ring[-1], 'narrow', [(dev, (dev + 1) % 8) for dev in range(8)])]
    all_gather x1 -> x0, waiting for transfers between devices: 26 us -> none  [shards(): whole_rows = lax.all_gather(hidden_out, 'narrow', axis=0, tiled=True)]
    unnamed x7 -> x6, waiting for transfers between devices: 32.2 us -> 32.3 us
  transfers between devices with their start and end apart: 6 -> 12, of which waited for: 5 -> 11; matrix products, arithmetic and copies ran while one was open for 1% -> 2% of each run, Pallas kernels for 0% -> 0%
where the time goes in v1:
time: 547 us; the launch traced here: 546 us
  waiting for transfers between devices  227 us (41%)
  blocking collectives  120 us (22%)
  local copies, waits for them, and re-layouts  102 us (19%)
  matrix products  50.8 us (9%)
  other arithmetic  29.4 us (5%)
  between operations  14 us (3%)
    all_gather x1, waiting for transfers between devices, shards(): value_rows = lax.all_gather(values, 'wide', axis=1, tiled=True)  82.1 us
    all_gather x1, blocking collectives, shards(): seg_rows = lax.all_gather(seg_packed, 'wide', axis=1, tiled=True)  51.9 us
    all_gather x1, blocking collectives, shards(): lax.all_gather(out_weight, 'wide', axis=1, tiled=True)  48.9 us
    ppermute x7, waiting for transfers between devices, shards(): lax.ppermute(ring[-1], 'narrow', [(dev, (dev + 1) % 8) for dev in range(8)])  45.3 us
    dynamic_slice x64, local copies, waits for them, and re-layouts, shards(): carry, unused = lax.scan(step_block, carry, stacked)  34.9 us
    all_gather x1, waiting for transfers between devices, shards(): lax.all_gather(merge_weight, 'wide', axis=2, tiled=True)  34.3 us
    reduce_scatter x1, waiting for transfers between devices, shards(): lax.psum_scatter(partial_mix.astype(jnp.bfloat16), 'narrow', scatter_dime...  32.8 us
    unnamed x6, waiting for transfers between devices  32.3 us
  transfers between devices with their start and end apart: 12, of which 11 were waited for; matrix products, arithmetic and copies ran while one was open for 2% of the time, Pallas kernels for 0%

profile of v1, /device:TPU:32, one launch (start us, length us, event | category | flops | bytes accessed | tf_op | source)
XLA Modules:
  0.0 546.1 jit_solution(9004640704300668794)
XLA Ops:
  9.7 51.9 %all_gather.15 = s32[1,1024,16]{2,0,1:T(1,128)S(1)} all-gather(s32[1,32,16]{2,0,1:T(1,128)S(1)} %copy.25), channel_id=1, replica_groups=mesh['wide'=32,'narrow'=8] {'wide'}, dimensions={1}, use_global_device_ids=true | all-gather | bytes 67584 | tf_op jit(solution)/shard_map/all_gather | solution.py:54
  62.1 2.0 reduce.3
  64.4 1.5 reshape.87
  66.0 48.9 %all-gather = bf16[32,52,208]{2,1,0:T(8,128)(2,1)S(1)} all-gather(bf16[1,52,208]{2,1,0:T(8,128)(2,1)S(1)} %bitcast.77), channel_id=1, replica_groups=mesh['wide'=32,'narrow'=8] {'wide'}, dimensions={0}, use_global_device_ids=true | all-gather | bytes 713856 | tf_op jit(solution)/shard_map/all_gather | solution.py:19
  114.9 1.3 reshape.93
  116.2 82.1 %all-gather.7.cloned.1.call-done = bf16[2,1024,1664]{2,1,0:T(8,128)(2,1)} async-done(((bf16[2,32,1664]{2,1,0:T(8,128)(2,1)}), bf16[2,1024,1664]{2,1,0:T(8,128)(2,1)}) %all-gather.7.cloned.1.call-update) | async-done | bytes 6815760 | tf_op jit(solution)/shard_map/all_gather | solution.py:53
  198.3 167.3 %while.15 = (s32[]{:T(128)}, f32[2,512]{1,0:T(2,128)S(1)}, f32[2,512]{1,0:T(2,128)S(1)}, f32[2,512,104]{1,2,0:T(8,128)S(1)}, s32[32,512]{1,0:T(8,128)S(1)}, /*in...) while((s32[]{:T(128)}, f32[2,512]{1,0:T(2,128)S(1)}, ...), condition=%wide.region_3.4_spmd.clone, body=%wide.region_0.3_spmd.clone.sunk | while | flops 225506304 | bytes 10615425 | solution.py:66
  199.4 1.1 dynamic-slice_bitcast_fusion.3
  204.6 1.1 dynamic-slice_bitcast_fusion.3
  209.9 1.1 dynamic-slice_bitcast_fusion.3
  215.1 1.1 dynamic-slice_bitcast_fusion.3
  220.3 1.1 dynamic-slice_bitcast_fusion.3
  225.5 1.1 dynamic-slice_bitcast_fusion.3
  230.8 1.1 dynamic-slice_bitcast_fusion.3
  236.0 1.1 dynamic-slice_bitcast_fusion.3
  241.2 1.1 dynamic-slice_bitcast_fusion.3
  246.5 1.1 dynamic-slice_bitcast_fusion.3
  251.7 1.1 dynamic-slice_bitcast_fusion.3
  256.9 1.1 dynamic-slice_bitcast_fusion.3
  262.1 1.1 dynamic-slice_bitcast_fusion.3
  267.4 1.1 dynamic-slice_bitcast_fusion.3
  272.6 1.1 dynamic-slice_bitcast_fusion.3
  277.8 1.1 dynamic-slice_bitcast_fusion.3
  283.1 1.1 dynamic-slice_bitcast_fusion.3
  288.3 1.1 dynamic-slice_bitcast_fusion.3
  293.5 1.1 dynamic-slice_bitcast_fusion.3
  298.8 1.1 dynamic-slice_bitcast_fusion.3
  304.0 1.1 dynamic-slice_bitcast_fusion.3
  309.2 1.1 dynamic-slice_bitcast_fusion.3
  314.4 1.1 dynamic-slice_bitcast_fusion.3
  319.7 1.1 dynamic-slice_bitcast_fusion.3
  324.9 1.1 dynamic-slice_bitcast_fusion.3
  330.1 1.1 dynamic-slice_bitcast_fusion.3
  335.4 1.1 dynamic-slice_bitcast_fusion.3
  340.6 1.1 dynamic-slice_bitcast_fusion.3
  365.7 3.1 convolution_convert_fusion
  369.5 32.8 %reduce-scatter.5.cloned.1.call-done = bf16[64,1664]{1,0:T(8,128)(2,1)} async-done(((bf16[512,1664]{1,0:T(8,128)(2,1)}), bf16[64,1664]{1,0:T(8,128)(2,1)}) %reduce-scatter.5.cloned.1.call-update) | async-done | bytes 213008 | tf_op jit(solution)/shard_map/reduce_scatter | solution.py:75
  403.3 6.5 %collective-permute-done = bf16[64,1664]{1,0:T(8,128)(2,1)S(1)} collective-permute-done((bf16[64,1664]{1,0:T(8,128)(2,1)S(1)}, bf16[64,1664]{1,0:T(8,128)(2,1)S(1)}, u32[]{:S(2)}, u32[]{:S(2)}) %collective-permute-start) | collective-permute-done | bytes 213024 | tf_op jit(solution)/shard_map/ppermute | solution.py:81
  409.7 6.5 %collective-permute-done.1 = bf16[64,1664]{1,0:T(8,128)(2,1)S(1)} collective-permute-done((bf16[64,1664]{1,0:T(8,128)(2,1)S(1)}, bf16[64,1664]{1,0:T(8,128)(2,1)S(1)}, u32[]{:S(2)}, u32[]{:S(2)}) %collective-permute-start.1) | collective-permute-done | bytes 213024 | tf_op jit(solution)/shard_map/ppermute | solution.py:81
  416.2 6.5 %collective-permute-done.2 = bf16[64,1664]{1,0:T(8,128)(2,1)S(1)} collective-permute-done((bf16[64,1664]{1,0:T(8,128)(2,1)S(1)}, bf16[64,1664]{1,0:T(8,128)(2,1)S(1)}, u32[]{:S(2)}, u32[]{:S(2)}) %collective-permute-start.2) | collective-permute-done | bytes 213024 | tf_op jit(solution)/shard_map/ppermute | solution.py:81
  422.7 6.5 %collective-permute-done.3 = bf16[64,1664]{1,0:T(8,128)(2,1)S(1)} collective-permute-done((bf16[64,1664]{1,0:T(8,128)(2,1)S(1)}, bf16[64,1664]{1,0:T(8,128)(2,1)S(1)}, u32[]{:S(2)}, u32[]{:S(2)}) %collective-permute-start.3) | collective-permute-done | bytes 213024 | tf_op jit(solution)/shard_map/ppermute | solution.py:81
  429.2 6.5 %collective-permute-done.4 = bf16[64,1664]{1,0:T(8,128)(2,1)S(1)} collective-permute-done((bf16[64,1664]{1,0:T(8,128)(2,1)S(1)}, bf16[64,1664]{1,0:T(8,128)(2,1)S(1)}, u32[]{:S(2)}, u32[]{:S(2)}) %collective-permute-start.4) | collective-permute-done | bytes 213024 | tf_op jit(solution)/shard_map/ppermute | solution.py:81
  435.7 6.5 %collective-permute-done.5 = bf16[64,1664]{1,0:T(8,128)(2,1)S(1)} collective-permute-done((bf16[64,1664]{1,0:T(8,128)(2,1)S(1)}, bf16[64,1664]{1,0:T(8,128)(2,1)S(1)}, u32[]{:S(2)}, u32[]{:S(2)}) %collective-permute-start.5) | collective-permute-done | bytes 213024 | tf_op jit(solution)/shard_map/ppermute | solution.py:81
  442.1 6.5 %collective-permute-done.6 = bf16[64,1664]{1,0:T(8,128)(2,1)S(1)} collective-permute-done((bf16[64,1664]{1,0:T(8,128)(2,1)S(1)}, bf16[64,1664]{1,0:T(8,128)(2,1)S(1)}, u32[]{:S(2)}, u32[]{:S(2)}) %collective-permute-start.6) | collective-permute-done | bytes 213024 | tf_op jit(solution)/shard_map/ppermute | solution.py:81
  449.4 34.3 %all-gather.9.cloned.1.call-done = bf16[4,208,1664]{1,0,2:T(4,128)(2,1)} async-done(((bf16[4,208,52]{1,0,2:T(4,128)(2,1)}), bf16[4,208,1664]{1,0,2:T(4,128)(2,1)}) %all-gather.9.cloned.1.call-update) | async-done | bytes 2768912 | tf_op jit(solution)/shard_map/all_gather | solution.py:20
  483.6 3.8 fusion.23
  487.9 30.3 %reduce-scatter.7.cloned.1.call-done = bf16[208,128]{1,0:T(8,128)(2,1)} async-done(((bf16[1664,128]{1,0:T(8,128)(2,1)}), bf16[208,128]{1,0:T(8,128)(2,1)}) %reduce-scatter.7.cloned.1.call-update) | async-done | bytes 53264
  519.3 19.5 %all_to_all.5 = bf16[32,8,208]{2,1,0:T(8,128)(2,1)S(1)} all-to-all(bf16[32,8,208]{2,1,0:T(8,128)(2,1)S(1)} %bitcast.71), channel_id=1, replica_groups=mesh['wide'=32,'narrow'=8] {'wide'}, dimensions={0} | all-to-all | bytes 212992 | tf_op jit(solution)/shard_map/all_to_all | solution.py:111
  (451 shorter events, 142.2 us)
Async XLA Ops:
  7.2 58.8 %copy-start.2 = (bf16[208,52]{0,1:T(8,128)(2,1)S(1)}, bf16[208,52]{0,1:T(8,128)(2,1)}, u32[]{:S(2)}) copy-start(bf16[208,52]{0,1:T(8,128)(2,1)} %param.14) | copy-start | bytes 64900
  7.2 109.1 %all-gather.5.cloned.1.call-start = ((), (), s32[]{:S(2)}) async-start(), calls=%async_computation.3 | async-start | bytes 7028736 | tf_op jit(solution)/shard_map/all_gather | solution.py:52
  7.9 190.4 %all-gather.7.cloned.1.call-start = ((), (), s32[]{:S(2)}) async-start(), calls=%async_computation.4 | async-start | bytes 7028736 | tf_op jit(solution)/shard_map/all_gather | solution.py:53
  8.7 393.6 %reduce-scatter.5.cloned.1.call-start = ((), (), s32[]{:S(2)}) async-start(), calls=%async_computation.5 | async-start | bytes 1916928 | tf_op jit(solution)/shard_map/reduce_scatter | solution.py:75
  365.6 36.6 %copy-start.1 = (bf16[64,1664]{1,0:T(8,128)(2,1)S(1)}, bf16[64,1664]{1,0:T(8,128)(2,1)}, u32[]{:S(2)}) copy-start(bf16[64,1664]{1,0:T(8,128)(2,1)} %param.10) | copy-start | bytes 638980
  368.8 114.8 %all-gather.9.cloned.1.call-start = ((), (), s32[]{:S(2)}) async-start(), calls=%async_computation.6 | async-start | bytes 3514368 | tf_op jit(solution)/shard_map/all_gather | solution.py:20
  369.4 148.8 %reduce-scatter.7.cloned.1.call-start = ((), (), s32[]{:S(2)}) async-start(), calls=%async_computation.7 | async-start | bytes 479232
  403.2 45.9 %copy-start = (bf16[64,1664]{1,0:T(8,128)(2,1)}, bf16[64,1664]{1,0:T(8,128)(2,1)S(1)}, u32[]{:S(2)}) copy-start(bf16[64,1664]{1,0:T(8,128)(2,1)S(1)} %add_convert_fusion) | copy-start | bytes 638980
  403.2 6.5 %collective-permute-start = (bf16[64,1664]{1,0:T(8,128)(2,1)S(1)}, bf16[64,1664]{1,0:T(8,128)(2,1)S(1)}, u32[]{:S(2)}, u32[]{:S(2)}) collective-permute-start(bf16[64,1664]{1,0:T(8,128)(2,1)S(1)} %add_convert_fusion), channel_id=1, source_target_pairs={{0,1},{1,2},{2,3},{3,4},{4,5},{5,6},{6,7},{7,0},{8,9},{9,10},{10,1... | collective-permute-start | bytes 638984 | tf_op jit(solution)/shard_map/ppermute | solution.py:81
  409.7 6.5 %collective-permute-start.1 = (bf16[64,1664]{1,0:T(8,128)(2,1)S(1)}, bf16[64,1664]{1,0:T(8,128)(2,1)S(1)}, u32[]{:S(2)}, u32[]{:S(2)}) collective-permute-start(bf16[64,1664]{1,0:T(8,128)(2,1)S(1)} %collective-permute-done), channel_id=1, source_target_pairs={{0,1},{1,2},{2,3},{3,4},{4,5},{5,6},{6,7},{7,0},{8,9},{9,10},{10,1... | collective-permute-start | bytes 638984 | tf_op jit(solution)/shard_map/ppermute | solution.py:81
  416.2 6.5 %collective-permute-start.2 = (bf16[64,1664]{1,0:T(8,128)(2,1)S(1)}, bf16[64,1664]{1,0:T(8,128)(2,1)S(1)}, u32[]{:S(2)}, u32[]{:S(2)}) collective-permute-start(bf16[64,1664]{1,0:T(8,128)(2,1)S(1)} %collective-permute-done.1), channel_id=1, source_target_pairs={{0,1},{1,2},{2,3},{3,4},{4,5},{5,6},{6,7},{7,0},{8,9},{9,10},{10,1... | collective-permute-start | bytes 638984 | tf_op jit(solution)/shard_map/ppermute | solution.py:81
  422.7 6.5 %collective-permute-start.3 = (bf16[64,1664]{1,0:T(8,128)(2,1)S(1)}, bf16[64,1664]{1,0:T(8,128)(2,1)S(1)}, u32[]{:S(2)}, u32[]{:S(2)}) collective-permute-start(bf16[64,1664]{1,0:T(8,128)(2,1)S(1)} %collective-permute-done.2), channel_id=1, source_target_pairs={{0,1},{1,2},{2,3},{3,4},{4,5},{5,6},{6,7},{7,0},{8,9},{9,10},{10,1... | collective-permute-start | bytes 638984 | tf_op jit(solution)/shard_map/ppermute | solution.py:81
  429.2 6.5 %collective-permute-start.4 = (bf16[64,1664]{1,0:T(8,128)(2,1)S(1)}, bf16[64,1664]{1,0:T(8,128)(2,1)S(1)}, u32[]{:S(2)}, u32[]{:S(2)}) collective-permute-start(bf16[64,1664]{1,0:T(8,128)(2,1)S(1)} %collective-permute-done.3), channel_id=1, source_target_pairs={{0,1},{1,2},{2,3},{3,4},{4,5},{5,6},{6,7},{7,0},{8,9},{9,10},{10,1... | collective-permute-start | bytes 638984 | tf_op jit(solution)/shard_map/ppermute | solution.py:81
  435.7 6.5 %collective-permute-start.5 = (bf16[64,1664]{1,0:T(8,128)(2,1)S(1)}, bf16[64,1664]{1,0:T(8,128)(2,1)S(1)}, u32[]{:S(2)}, u32[]{:S(2)}) collective-permute-start(bf16[64,1664]{1,0:T(8,128)(2,1)S(1)} %collective-permute-done.4), channel_id=1, source_target_pairs={{0,1},{1,2},{2,3},{3,4},{4,5},{5,6},{6,7},{7,0},{8,9},{9,10},{10,1... | collective-permute-start | bytes 638984 | tf_op jit(solution)/shard_map/ppermute | solution.py:81
  442.1 6.5 %collective-permute-start.6 = (bf16[64,1664]{1,0:T(8,128)(2,1)S(1)}, bf16[64,1664]{1,0:T(8,128)(2,1)S(1)}, u32[]{:S(2)}, u32[]{:S(2)}) collective-permute-start(bf16[64,1664]{1,0:T(8,128)(2,1)S(1)} %collective-permute-done.5), channel_id=1, source_target_pairs={{0,1},{1,2},{2,3},{3,4},{4,5},{5,6},{6,7},{7,0},{8,9},{9,10},{10,1... | collective-permute-start | bytes 638984 | tf_op jit(solution)/shard_map/ppermute | solution.py:81
  449.0 38.4 %copy-start.3 = (s32[128,1]{0,1:T(1,128)S(1)}, s32[128,1]{0,1:T(1,128)}, u32[]{:S(2)}) copy-start(s32[128,1]{0,1:T(1,128)} %param.17) | copy-start | bytes 1540
Sparse Core Ops, SparseCore 0:
  10.6 96.2 all-gather.4
  109.5 88.7 all-gather.6
  369.0 33.2 reduce-scatter.4
  405.0 78.5 all-gather.8
  487.6 30.6 reduce-scatter.6
